TPU v7x, 32 devices: a whole 2x2x4 slice. The times are simulated.
32 devices in a mesh: rep: 2 (over x), idx: 16 (over z, y, core).
Axes of the slice: x: 2, y: 2, z: 4, core: 2. Of those that a mesh axis runs over, the one named last changes fastest.
Arguments:
- images: bfloat16 [16448, 1408], P(('rep', 'idx')), parts along dimension 0, may hold values from -6 to 6
- norm_gain: float32 [1408], replicated, may hold values from 0.25 to 1.75
- qkv_values: bfloat16 [1408, 4224], P(None, 'idx'), may hold values from -0.5 to 0.5
- qkv_exponents: int32 [11, 4224], replicated, may hold values from -2 to 2
- proj_values: bfloat16 [1408, 1408], P(None, 'idx'), may hold values from -0.078125 to 0.078125
- proj_exponents: int32 [11, 1408], replicated, may hold values from -2 to 2
- captions: bfloat16 [32768, 1408], P(('rep', 'idx')), parts along dimension 0, may hold values from -0.15625 to 0.15625
- owners: int32 [16448, 1], P(('rep', 'idx')), parts along dimension 0, may hold values from 0 to 15; in each aligned block of 514 rows (0 to 513, 514 to 1027, ...) at most 34 rows name the same one
- candidates: int32 [16448, 4], P(('rep', 'idx')), parts along dimension 0, may hold values from 0 to 7, all different within a row
Outputs:
- embedding: bfloat16 [16448, 1408], P(('rep', 'idx')), parts along dimension 0
- scores: bfloat16 [16448, 4, 128], P(('rep', 'idx')), parts along dimension 0
There are 2 independent parts, one for each index of `rep`. A program takes and returns all parts, laid end to end along the dimension named above; an argument that names none is the same for every part. Nothing has to cross between parts.
Inputs may be any that keep to these rules, and one draw needn't show every extreme that they name: `owners`: among the tokens of one device no owner is named more than 34 times, a bound that some block reaches. `candidates`: each token names 4 different caption blocks.
All inputs are finite; a program needn't handle non-finite values.
Results may differ from a plain program's by a relative error of at most 0.004.
The roundings to bfloat16 on the way count: a program that leaves them out, or rounds other values in their place, can miss the bound.
Values may be sent and summed in bfloat16 or wider, within the bound.
A program may use at most 192 MiB of HBM per device.

v0:
```python
import jax
import jax.numpy as jnp
from jax import lax
from jax.sharding import PartitionSpec as P

HEADS = 16
PATCHES = 257
CBLK = 8
CAPT = 128


def dequant(stored, exponents):
    row_count, col_count = stored.shape
    block_count = exponents.shape[0]
    scaled = stored.astype(jnp.float32).reshape(block_count, row_count // block_count, col_count)
    scaled = scaled * jnp.exp2(exponents.astype(jnp.float32))[:, None, :]
    return scaled.reshape(row_count, col_count).astype(jnp.bfloat16)


def layer_norm(token_rows, norm_gain):
    values = token_rows.astype(jnp.float32)
    centered = values - jnp.mean(values, axis=-1, keepdims=True)
    inv_scale = lax.rsqrt(jnp.mean(centered * centered, axis=-1, keepdims=True) + 1e-06)
    return (centered * inv_scale * norm_gain).astype(jnp.bfloat16)


def attend(qkv_rows, model_width):
    head_dim = model_width // HEADS
    grouped = qkv_rows.reshape(-1, PATCHES, 3, HEADS, head_dim)
    logits = jnp.einsum(
        "gqhd,gkhd->ghqk", grouped[:, :, 0], grouped[:, :, 1], preferred_element_type=jnp.float32
    )
    logits = logits * head_dim ** (-0.5)
    logits = logits - jnp.max(logits, axis=-1, keepdims=True)
    weights = jnp.exp(logits)
    attn_probs = (weights / jnp.sum(weights, axis=-1, keepdims=True)).astype(jnp.bfloat16)
    mixed_heads = jnp.einsum(
        "ghqk,gkhd->gqhd", attn_probs, grouped[:, :, 2], preferred_element_type=jnp.float32
    )
    return mixed_heads.astype(jnp.bfloat16).reshape(-1, model_width)


def project_with(left_rows, exponents, col_piece):
    return jnp.dot(left_rows, dequant(col_piece, exponents), preferred_element_type=jnp.float32)


def score_with(captions):

    def score_slots(slot_parts):
        slot_rows, slot_picks = slot_parts
        peer_count, item_count = (slot_rows.shape[0], slot_rows.shape[1])
        flat_rows = slot_rows.reshape(peer_count * item_count, slot_rows.shape[2])
        all_scores = lax.dot_general(
            flat_rows, captions, (((1,), (1,)), ((), ())), preferred_element_type=jnp.float32
        )
        all_scores = all_scores.reshape(peer_count * item_count, CBLK, CAPT)
        block_index = jnp.clip(
            slot_picks.reshape(peer_count * item_count, -1).astype(jnp.int32), 0, CBLK - 1
        )
        chosen = jnp.take_along_axis(all_scores, block_index[:, :, None], axis=1)
        return chosen.astype(jnp.bfloat16).reshape(peer_count, item_count, -1, CAPT)

    return score_slots


def local(
    images,
    norm_gain,
    qkv_values,
    qkv_exponents,
    proj_values,
    proj_exponents,
    captions,
    owners,
    candidates,
):
    model_width = images.shape[1]
    normed = layer_norm(images, norm_gain)
    qkv_rows = project_with(
        normed, qkv_exponents, lax.all_gather(qkv_values, "idx", axis=1, tiled=True)
    ).astype(jnp.bfloat16)
    mixed_heads = attend(qkv_rows, model_width)
    branch = project_with(
        mixed_heads, proj_exponents, lax.all_gather(proj_values, "idx", axis=1, tiled=True)
    )
    hidden = images.astype(jnp.float32) + branch
    inv_scale = lax.rsqrt(jnp.mean(hidden * hidden, axis=-1, keepdims=True) + 1e-06)
    embedding = (hidden * inv_scale).astype(jnp.bfloat16)
    token_count = embedding.shape[0]
    peer_count = lax.axis_size("idx")
    capacity = (token_count + peer_count - 1) // peer_count + 1
    owner_ids = owners[:, 0]
    onehot = (owner_ids[:, None] == jnp.arange(peer_count, dtype=jnp.int32)[None, :]).astype(
        jnp.int32
    )
    slot_rank = jnp.sum((jnp.cumsum(onehot, axis=0) - onehot) * onehot, axis=1)
    slot_index = owner_ids * capacity + slot_rank
    send_rows = (
        jnp.zeros((peer_count * capacity, model_width), jnp.bfloat16).at[slot_index].set(embedding)
    )
    send_rows = send_rows.reshape(peer_count, capacity, model_width)
    pick_count = candidates.shape[1]
    send_picks = (
        jnp.full((peer_count * capacity, pick_count), -1.0, jnp.bfloat16)
        .at[slot_index]
        .set(candidates.astype(jnp.bfloat16))
    )
    send_picks = send_picks.reshape(peer_count, capacity, pick_count)
    score_slots = score_with(captions)
    arrived = (
        lax.all_to_all(send_rows, "idx", split_axis=0, concat_axis=0, tiled=True),
        lax.all_to_all(send_picks, "idx", split_axis=0, concat_axis=0, tiled=True),
    )
    returned = lax.all_to_all(score_slots(arrived), "idx", split_axis=0, concat_axis=0, tiled=True)
    scores = returned.reshape(peer_count * capacity, pick_count, CAPT)[slot_index]
    return (embedding, scores)


def solution(mesh):
    placed = (
        P(("rep", "idx"), None),
        P(),
        P(None, "idx"),
        P(),
        P(None, "idx"),
        P(),
        P(("rep", "idx"), None),
        P(("rep", "idx"), None),
        P(("rep", "idx"), None),
    )
    return jax.shard_map(
        local,
        mesh=mesh,
        in_specs=placed,
        out_specs=(P(("rep", "idx"), None), P(("rep", "idx"), None, None)),
        check_vma=False,
    )
```

profile of v0, /device:TPU:0, one launch (start us, length us, event | category | flops | bytes accessed | tf_op | source)
XLA Modules:
  0.0 386.5 jit_solution(72550061638257239)
XLA Ops:
  12.8 4.2 %scatter_custom_fusion = bf16[544,4]{1,0:T(8,128)(2,1)S(1)} fusion(s32[514]{0:T(1024)S(1)} %fusion.30, bf16[514,4]{1,0:T(8,128)(2,1)S(1)} %copy.41, bf16[]{:T(256)} %constant.14.clone.1), kind=kCustom, calls=%fused_computation.40 | custom fusion | bytes 4354 | tf_op jit(solution)/shard_map/scatter | solution.py:106
  17.9 7.4 %all-to-all-start = ((bf16[16,34,4]{1,2,0:T(4,128)(2,1)}), bf16[16,34,4]{1,2,0:T(4,128)(2,1)S(1)}, u32[]{:S(2)}, u32[]{:S(2)}) async-start(bf16[16,34,4]{1,2,0:T(4,128)(2,1)} %copy.43), calls=%async_computation | async-start | bytes 32768 | tf_op jit(solution)/shard_map/all_to_all | solution.py:112
  29.1 33.5 %all-gather.5.cloned.1.call-done = bf16[1408,1408]{0,1:T(8,128)(2,1)} async-done(((bf16[1408,88]{0,1:T(8,128)(2,1)}), bf16[1408,1408]{0,1:T(8,128)(2,1)}) %all-gather.5.cloned.1.call-update) | async-done | bytes 3964944 | tf_op jit(solution)/shard_map/all_gather | solution.py:84
  62.6 6.2 %copy.38 = bf16[1408,1408]{1,0:T(8,128)(2,1)} copy(bf16[1408,1408]{0,1:T(8,128)(2,1)} %all-gather.5.cloned.1.call-done) | data formatting | bytes 7929856 | tf_op jit(solution)/shard_map/all_gather | solution.py:84
  68.8 5.0 %fusion.5 = bf16[1408,1408]{1,0:T(8,128)(2,1)} fusion(bf16[1408,1408]{1,0:T(8,128)(2,1)} %copy.38, f32[11,1408]{1,0:T(8,128)S(1)} %multiply_exponential_fusion.1), kind=kLoop, calls=%fused_computation.12 | loop fusion | flops 5947392 | bytes 7991808 | tf_op jit(solution)/shard_map/convert_element_type | solution.py:17
  73.8 85.8 %all-gather.3.cloned.1.call-done = bf16[1408,4224]{0,1:T(8,128)(2,1)} async-done(((bf16[1408,264]{0,1:T(8,128)(2,1)}), bf16[1408,4224]{0,1:T(8,128)(2,1)}) %all-gather.3.cloned.1.call-update) | async-done | bytes 11894800 | tf_op jit(solution)/shard_map/all_gather | solution.py:80
  159.6 16.0 %copy.32 = bf16[1408,4224]{1,0:T(8,128)(2,1)} copy(bf16[1408,4224]{0,1:T(8,128)(2,1)} %all-gather.3.cloned.1.call-done) | data formatting | bytes 23789568 | tf_op jit(solution)/shard_map/all_gather | solution.py:80
  175.6 6.8 %fusion.1 = bf16[1408,4224]{1,0:T(8,128)(2,1)S(1)} fusion(bf16[1408,4224]{1,0:T(8,128)(2,1)} %copy.32, f32[11,4224]{1,0:T(8,128)S(1)} %multiply_exponential_fusion), kind=kLoop, calls=%fused_computation.6 | loop fusion | flops 17842176 | bytes 23975424 | tf_op jit(solution)/shard_map/convert_element_type | solution.py:17
  182.4 9.2 %convolution_convert_fusion = bf16[514,4224]{1,0:T(8,128)(2,1)} fusion(bf16[1408,4224]{1,0:T(8,128)(2,1)S(1)} %fusion.1, bf16[514,1408]{1,0:T(8,128)(2,1)S(1)} %copy-done.1, f32[1408]{0:T(1024)S(1)} %copy-done.4, f32[514]{0:T(1024)S(1)} %add_rsqrt_fusion.1, f32[514]{0:T(1024)S(1)} %broadcast_multiply_fusion), kind=kOutput, calls=%fused_computation.13 | convolution fusion | flops 6119708672 | bytes 17694224 | tf_op jit(solution)/shard_map/dot_general | solution.py:44
  191.6 14.7 %reshape.106 = bf16[2,257,3,16,88]{4,3,2,1,0:T(8,128)(2,1)} reshape(bf16[514,4224]{1,0:T(8,128)(2,1)} %convolution_convert_fusion) | data formatting | bytes 8684544 | tf_op jit(solution)/shard_map/reshape | solution.py:29
  206.2 5.3 %fusion.32 = (bf16[2,257,1,16,88]{4,3,2,1,0:T(8,128)(2,1)}, bf16[2,257,1,16,88]{4,3,2,1,0:T(8,128)(2,1)S(1)}, bf16[2,257,1,16,88]{4,3,2,1,0:T(8,128)(2,1)S(1)}) fusion(bf16[2,257,3,16,88]{4,3,2,1,0:T(8,128)(2,1)} %reshape.106), kind=kLoop, calls=%fused_computation.65 | loop fusion | bytes 8684544 | tf_op jit(solution)/shard_map/slice | solution.py:38
  211.5 7.2 %fusion.13 = f32[2,16,257,257]{2,3,1,0:T(8,128)} fusion(bf16[2,257,1,16,88]{4,3,2,1,0:T(8,128)(2,1)S(1)} %get-tuple-element.3, bf16[2,257,1,16,88]{4,3,2,1,0:T(8,128)(2,1)S(1)} %get-tuple-element.4), kind=kOutput, calls=%fused_computation.27 | convolution fusion | flops 371987968 | bytes 11349120 | tf_op jit(solution)/shard_map/gqhd,gkhd->ghqk/dot_general | solution.py:30
  218.7 16.6 %fusion.33 = (f32[2,16,257]{2,1,0:T(8,128)S(1)}, f32[2,16,257,257]{2,3,1,0:T(8,128)}) fusion(f32[2,16,257,257]{2,3,1,0:T(8,128)} %fusion.13), kind=kOutput, calls=%fused_computation.66 | output fusion | flops 8454528 | bytes 16941440 | tf_op jit(solution)/shard_map/sub | solution.py:34
  235.3 4.4 %copy.49 = bf16[2,257,1,16,88]{1,4,3,0,2:T(8,128)(2,1)} copy(bf16[2,257,1,16,88]{4,3,2,1,0:T(8,128)(2,1)} %get-tuple-element.2) | data formatting | bytes 2894848
  239.8 8.5 %convert_bitcast_fusion = bf16[2,257,16,88]{1,3,2,0:T(8,128)(2,1)} fusion(f32[2,16,257,257]{2,3,1,0:T(8,128)} %get-tuple-element.6, f32[2,16,257]{2,1,0:T(8,128)S(1)} %get-tuple-element.5, bf16[2,257,1,16,88]{1,4,3,0,2:T(8,128)(2,1)} %copy.49), kind=kOutput, calls=%fused_computation.30 | convolution fusion | flops 376938816 | bytes 11382016 | tf_op jit(solution)/shard_map/ghqk,gkhd->gqhd/dot_general | solution.py:37
  248.3 4.5 %copy.37 = bf16[2,257,16,88]{3,2,1,0:T(8,128)(2,1)} copy(bf16[2,257,16,88]{1,3,2,0:T(8,128)(2,1)} %convert_bitcast_fusion) | data formatting | bytes 2894848 | tf_op jit(solution)/shard_map/convert_element_type | solution.py:40
  252.8 4.6 %reshape.107 = bf16[514,1408]{1,0:T(8,128)(2,1)} reshape(bf16[2,257,16,88]{3,2,1,0:T(8,128)(2,1)} %copy.37) | data formatting | bytes 2894848 | tf_op jit(solution)/shard_map/reshape | solution.py:40
  257.5 7.3 %multiply_reduce_fusion.1 = (f32[514]{0:T(1024)S(1)}, f32[514,1408]{1,0:T(8,128)}) fusion(bf16[514,1408]{1,0:T(8,128)(2,1)} %reshape.107, bf16[1408,1408]{1,0:T(8,128)(2,1)} %fusion.5, bf16[514,1408]{1,0:T(8,128)(2,1)} %param.9), kind=kOutput, calls=%fused_computation.25 | convolution fusion | flops 2040867328 | bytes 9756680 | tf_op jit(solution)/shard_map/dot_general | solution.py:44
  264.7 12.3 %scatter_custom_fusion.1 = bf16[544,1408]{1,0:T(8,128)(2,1)} fusion(s32[514]{0:T(1024)S(1)} %fusion.30, bf16[]{:T(256)} %constant.45.clone.1, f32[514,1408]{1,0:T(8,128)} %get-tuple-element.8, f32[514]{0:T(1024)S(1)} %add_rsqrt_fusion), kind=kCustom, calls=%fused_computation.35 | custom fusion | flops 1447424 | bytes 4430850 | tf_op jit(solution)/shard_map/scatter | solution.py:99
  279.6 4.4 %all-to-all-start.1 = ((bf16[16,34,1408]{2,1,0:T(8,128)(2,1)}), bf16[16,34,1408]{2,1,0:T(8,128)(2,1)}, u32[]{:S(2)}, u32[]{:S(2)}) async-start(bf16[16,34,1408]{2,1,0:T(8,128)(2,1)} %reshape.111), calls=%async_computation.1 | async-start | bytes 3604480 | tf_op jit(solution)/shard_map/all_to_all | solution.py:111
  284.9 35.0 %all-to-all-done.1 = bf16[16,34,1408]{2,1,0:T(8,128)(2,1)} async-done(((bf16[16,34,1408]{2,1,0:T(8,128)(2,1)}), bf16[16,34,1408]{2,1,0:T(8,128)(2,1)}, u32[]{:S(2)}, u32[]{:S(2)}) %all-to-all-start.1) | async-done | bytes 1531936 | tf_op jit(solution)/shard_map/all_to_all | solution.py:111
  327.2 23.0 %gather_fusion.1 = bf16[2176,128]{1,0:T(8,128)(2,1)S(1)} fusion(bf16[544,8,128]{2,1,0:T(8,128)(2,1)} %copy.47, s32[2176]{0:T(1024)S(1)} %reshape.123), kind=kCustom, calls=%fused_computation.1 | custom fusion | bytes 1131520 | tf_op jit(solution)/shard_map/jit(take_along_axis)/gather | solution.py:60
  351.7 10.1 %all-to-all-start.2 = ((bf16[16,34,4,128]{3,2,1,0:T(4,128)(2,1)}), bf16[16,34,4,128]{3,2,1,0:T(4,128)(2,1)S(1)}, u32[]{:S(2)}, u32[]{:S(2)}) async-start(bf16[16,34,4,128]{3,2,1,0:T(4,128)(2,1)} %select_convert_fusion), calls=%async_computation.2 | async-start | bytes 1114112 | tf_op jit(solution)/shard_map/all_to_all | solution.py:114
  364.9 11.6 %all-to-all-done.2 = bf16[16,34,4,128]{3,2,1,0:T(4,128)(2,1)S(1)} async-done(((bf16[16,34,4,128]{3,2,1,0:T(4,128)(2,1)}), bf16[16,34,4,128]{3,2,1,0:T(4,128)(2,1)S(1)}, u32[]{:S(2)}, u32[]{:S(2)}) %all-to-all-start.2) | async-done | bytes 557088 | tf_op jit(solution)/shard_map/all_to_all | solution.py:114
  (52 shorter events, 28.5 us)
Async XLA Ops:
  7.2 315.3 %copy-start = (bf16[1024,1408]{1,0:T(8,128)(2,1)S(1)}, bf16[1024,1408]{1,0:T(8,128)(2,1)}, u32[]{:S(2)}) copy-start(bf16[1024,1408]{1,0:T(8,128)(2,1)} %param.15) | copy-start | bytes 8650756
  7.2 21.8 %copy-start.2 = (s32[11,4224]{1,0:T(8,128)S(1)}, s32[11,4224]{1,0:T(8,128)}, u32[]{:S(2)}) copy-start(s32[11,4224]{1,0:T(8,128)} %param.12) | copy-start | bytes 557572
  7.2 55.4 %all-gather.5.cloned.1.call-start = ((), (), s32[]{:S(2)}) async-start(), calls=%async_computation.4 | async-start | bytes 4212736 | tf_op jit(solution)/shard_map/all_gather | solution.py:84
  7.9 151.7 %all-gather.3.cloned.1.call-start = ((), (), s32[]{:S(2)}) async-start(), calls=%async_computation.3 | async-start | bytes 12638208 | tf_op jit(solution)/shard_map/all_gather | solution.py:80
  17.1 11.9 %copy-start.3 = (s32[11,1408]{1,0:T(8,128)S(1)}, s32[11,1408]{1,0:T(8,128)}, u32[]{:S(2)}) copy-start(s32[11,1408]{1,0:T(8,128)} %param.14) | copy-start | bytes 185860
  17.9 261.7 %all-to-all-start = ((bf16[16,34,4]{1,2,0:T(4,128)(2,1)}), bf16[16,34,4]{1,2,0:T(4,128)(2,1)S(1)}, u32[]{:S(2)}, u32[]{:S(2)}) async-start(bf16[16,34,4]{1,2,0:T(4,128)(2,1)} %copy.43), calls=%async_computation | async-start | bytes 32768 | tf_op jit(solution)/shard_map/all_to_all | solution.py:112
  175.5 6.8 %copy-start.1 = (bf16[514,1408]{1,0:T(8,128)(2,1)S(1)}, bf16[514,1408]{1,0:T(8,128)(2,1)}, u32[]{:S(2)}) copy-start(bf16[514,1408]{1,0:T(8,128)(2,1)} %param.9) | copy-start | bytes 4342276
  175.6 6.8 %copy-start.4 = (f32[1408]{0:T(1024)S(1)}, f32[1408]{0:T(1024)}, u32[]{:S(2)}) copy-start(f32[1408]{0:T(1024)} %param.10) | copy-start | bytes 16900
  279.6 40.3 %all-to-all-start.1 = ((bf16[16,34,1408]{2,1,0:T(8,128)(2,1)}), bf16[16,34,1408]{2,1,0:T(8,128)(2,1)}, u32[]{:S(2)}, u32[]{:S(2)}) async-start(bf16[16,34,1408]{2,1,0:T(8,128)(2,1)} %reshape.111), calls=%async_computation.1 | async-start | bytes 3604480 | tf_op jit(solution)/shard_map/all_to_all | solution.py:111
  351.7 24.9 %all-to-all-start.2 = ((bf16[16,34,4,128]{3,2,1,0:T(4,128)(2,1)}), bf16[16,34,4,128]{3,2,1,0:T(4,128)(2,1)S(1)}, u32[]{:S(2)}, u32[]{:S(2)}) async-start(bf16[16,34,4,128]{3,2,1,0:T(4,128)(2,1)} %select_convert_fusion), calls=%async_computation.2 | async-start | bytes 1114112 | tf_op jit(solution)/shard_map/all_to_all | solution.py:114
Sparse Core Ops, SparseCore 0:
  10.2 52.3 all-gather.4
  64.7 94.8 all-gather.2
where the time goes:
time: 388 us; the launch traced here: 387 us
  waiting for transfers between devices  167 us (43%)
  local copies, waits for them, and re-layouts  94.7 us (24%)
  other arithmetic  52.8 us (14%)
  matrix products  35.4 us (9%)
  starting transfers between devices  22 us (6%)
  between operations  14.3 us (4%)
    all_gather x1, waiting for transfers between devices, local(): lax.all_gather(qkv_values, 'idx', axis=1, tiled=True)  85.8 us
    all_to_all x1, waiting for transfers between devices, local(): lax.all_to_all(send_rows, 'idx', split_axis=0, concat_axis=0, tiled=True)  35 us
    all_gather x1, waiting for transfers between devices, local(): lax.all_gather(proj_values, 'idx', axis=1, tiled=True)  33.5 us
    gather x3, local copies, waits for them, and re-layouts, score_slots(): chosen = jnp.take_along_axis(all_scores, block_index[:, :, None], axis=1)  23.3 us
    sub x1, other arithmetic, attend(): logits = logits - jnp.max(logits, axis=-1, keepdims=True)  16.6 us
    dot_general x2, matrix products, project_with(): jnp.dot(left_rows, dequant(col_piece, exponents), preferred_element_type=...  16.4 us
    all_gather x1, local copies, waits for them, and re-layouts, local(): lax.all_gather(qkv_values, 'idx', axis=1, tiled=True)  16 us
    reshape x1, local copies, waits for them, and re-layouts, attend(): grouped = qkv_rows.reshape(-1, PATCHES, 3, HEADS, head_dim)  14.7 us
  transfers between devices with their start and end apart: 5, of which 4 were waited for; matrix products, arithmetic and copies ran while one was open for 38% of the time, Pallas kernels for 0%

commit v1 on v0

v1 whole, which is shorter than its diff:
```python
import functools
import jax
import jax.numpy as jnp
from jax import lax
from jax.experimental import pallas as pl
from jax.experimental.pallas import tpu as pltpu
from jax.sharding import PartitionSpec as P

HEADS = 16
PATCHES = 257
CBLK = 8
CAPT = 128
F32 = jnp.float32
BF16 = jnp.bfloat16
VMEM = pltpu.VMEM
VLIMIT = 60 * 1024 * 1024


def dequant_rows(stored, exponents):
    row_count, col_count = stored.shape
    block_count = exponents.shape[0]
    turned = stored.T.astype(F32).reshape(col_count, block_count, row_count // block_count)
    scaled = turned * jnp.exp2(exponents.astype(F32)).T[:, :, None]
    return scaled.reshape(col_count, row_count).astype(BF16)


def layer_norm(token_rows, norm_gain):
    values = token_rows.astype(F32)
    centered = values - jnp.mean(values, axis=-1, keepdims=True)
    inv_scale = lax.rsqrt(jnp.mean(centered * centered, axis=-1, keepdims=True) + 1e-06)
    return (centered * inv_scale * norm_gain).astype(BF16)


def dot_nt(left, right):
    return lax.dot_general(left, right, (((1,), (1,)), ((), ())), preferred_element_type=F32)


def qkv_kernel(images_ref, gain_ref, w_ref, out_ref, normed):
    group, unit, head_dim = out_ref.shape[0], out_ref.shape[1], out_ref.shape[2]

    @pl.when(pl.program_id(0) == 0)
    def _():
        for g in range(group):
            normed[g] = layer_norm(images_ref[g], gain_ref[...])

    for g in range(group):
        rows = dot_nt(w_ref[...], normed[g])
        out_ref[g] = rows.reshape(unit, head_dim, rows.shape[1]).astype(BF16)


def qkv_call(images3, gain, w_rows):
    group, patches, width = images3.shape
    head_dim = width // HEADS
    units = w_rows.shape[0] // head_dim
    step = 4
    return pl.pallas_call(
        qkv_kernel,
        grid=(units // step,),
        in_specs=[
            pl.BlockSpec((group, patches, width), lambda i: (0, 0, 0)),
            pl.BlockSpec((1, width), lambda i: (0, 0)),
            pl.BlockSpec((step * head_dim, width), lambda i: (i, 0)),
        ],
        out_specs=pl.BlockSpec((group, step, head_dim, patches), lambda i: (0, i, 0, 0)),
        out_shape=jax.ShapeDtypeStruct((group, units, head_dim, patches), BF16),
        scratch_shapes=[pltpu.VMEM((group, patches, width), BF16)],
        compiler_params=pltpu.CompilerParams(vmem_limit_bytes=VLIMIT),
        name="qkv",
    )(images3, gain, w_rows)


def attend_kernel(qkv_ref, proj_ref, images_ref, slot_ref, emb_ref, send_ref, mixed):
    group, units, head_dim, patches = qkv_ref.shape
    width = HEADS * head_dim
    scale = head_dim ** (-0.5)
    for g in range(group):

        @pl.loop(0, HEADS)
        def _(h):
            queries, keys, vals = qkv_ref[g, h], qkv_ref[g, HEADS + h], qkv_ref[g, 2 * HEADS + h]
            logits = lax.dot_general(
                keys, queries, (((0,), (0,)), ((), ())), preferred_element_type=F32
            )
            logits = logits * scale
            weights = jnp.exp(logits - jnp.max(logits, axis=0, keepdims=True))
            probs = weights * (1.0 / jnp.sum(weights, axis=0, keepdims=True))
            out = jnp.dot(vals, probs.astype(BF16), preferred_element_type=F32)
            mixed[pl.ds(pl.multiple_of(h * head_dim, 8), head_dim), :] = out

        left = mixed[...].T.astype(BF16)
        hidden = images_ref[g].astype(F32) + dot_nt(left, proj_ref[...])
        inv_scale = lax.rsqrt(jnp.mean(hidden * hidden, axis=-1, keepdims=True) + 1e-06)
        emb_ref[g * patches:(g + 1) * patches, :] = (hidden * inv_scale).astype(BF16)
    slots = send_ref.shape[0]
    tokens = group * patches
    pick = lax.broadcasted_iota(jnp.int32, (slots, tokens), 0) == slot_ref[...]
    onehot = jnp.where(pick, 1.0, 0.0).astype(BF16)
    send_ref[...] = jnp.dot(onehot, emb_ref[...], preferred_element_type=F32).astype(BF16)


def attend_call(qkv, w_proj, images3, slot_row, slots):
    group, patches, width = images3.shape
    full = pl.BlockSpec(memory_space=VMEM)
    return pl.pallas_call(
        attend_kernel,
        in_specs=[full] * 4,
        out_specs=(full, full),
        out_shape=(
            jax.ShapeDtypeStruct((group * patches, width), BF16),
            jax.ShapeDtypeStruct((slots, width), BF16),
        ),
        scratch_shapes=[pltpu.VMEM((width, patches), F32)],
        compiler_params=pltpu.CompilerParams(vmem_limit_bytes=VLIMIT),
        name="attend",
    )(qkv, w_proj, images3, slot_row)


def score_kernel(rows_ref, picks_ref, captions_ref, out_ref):
    every = dot_nt(rows_ref[...], captions_ref[...]).astype(BF16)
    for k in range(picks_ref.shape[1]):
        pick = picks_ref[:, k:k + 1].astype(F32)
        chosen = jnp.zeros((every.shape[0], CAPT), F32)
        for b in range(CBLK):
            block = every[:, b * CAPT:(b + 1) * CAPT].astype(F32)
            chosen = jnp.where(pick == float(b), block, chosen)
        out_ref[:, k * CAPT:(k + 1) * CAPT] = chosen.astype(BF16)


def score_call(rows, picks, captions):
    full = pl.BlockSpec(memory_space=VMEM)
    return pl.pallas_call(
        score_kernel,
        in_specs=[full] * 3,
        out_specs=full,
        out_shape=jax.ShapeDtypeStruct((rows.shape[0], picks.shape[1] * CAPT), BF16),
        compiler_params=pltpu.CompilerParams(vmem_limit_bytes=VLIMIT),
        name="score",
    )(rows, picks, captions)


def return_kernel(slot_ref, rows_ref, out_ref):
    tokens, slots = out_ref.shape[0], rows_ref.shape[0]
    pick = lax.broadcasted_iota(jnp.int32, (tokens, slots), 1) == slot_ref[...]
    onehot = jnp.where(pick, 1.0, 0.0).astype(BF16)
    got = jnp.dot(onehot, rows_ref[...], preferred_element_type=F32).astype(BF16)
    for k in range(out_ref.shape[1]):
        out_ref[:, k, :] = got[:, k * CAPT:(k + 1) * CAPT]


def return_call(slot_col, rows, pick_count):
    full = pl.BlockSpec(memory_space=VMEM)
    return pl.pallas_call(
        return_kernel,
        in_specs=[full] * 2,
        out_specs=full,
        out_shape=jax.ShapeDtypeStruct((slot_col.shape[0], pick_count, CAPT), BF16),
        compiler_params=pltpu.CompilerParams(vmem_limit_bytes=VLIMIT),
        name="give_back",
    )(slot_col, rows)


def local(
    images,
    norm_gain,
    qkv_values,
    qkv_exponents,
    proj_values,
    proj_exponents,
    captions,
    owners,
    candidates,
):
    token_count, width = images.shape
    peer_count = lax.axis_size("idx")
    me = lax.axis_index("idx")
    capacity = (token_count + peer_count - 1) // peer_count + 1

    def own_exponents(exponents, cols):
        return lax.dynamic_slice_in_dim(exponents, me * cols, cols, axis=1)

    qkv_cols, proj_cols = qkv_values.shape[1], proj_values.shape[1]
    qkv_own = dequant_rows(qkv_values, own_exponents(qkv_exponents, qkv_cols))
    proj_own = dequant_rows(proj_values, own_exponents(proj_exponents, proj_cols))
    w_qkv = lax.all_gather(qkv_own, "idx", axis=0, tiled=True)
    w_proj = lax.all_gather(proj_own, "idx", axis=0, tiled=True)

    owner_ids = owners[:, 0]
    onehot = (owner_ids[:, None] == jnp.arange(peer_count, dtype=jnp.int32)[None, :]).astype(
        jnp.int32
    )
    slot_rank = jnp.sum((jnp.cumsum(onehot, axis=0) - onehot) * onehot, axis=1)
    slot_index = owner_ids * capacity + slot_rank
    slots = peer_count * capacity
    pick_count = candidates.shape[1]
    dispatch = (jnp.arange(slots, dtype=jnp.int32)[:, None] == slot_index[None, :]).astype(BF16)
    send_picks = jnp.dot(dispatch, candidates.astype(BF16), preferred_element_type=F32).astype(BF16)
    got_picks = lax.all_to_all(
        send_picks.reshape(peer_count, capacity, pick_count), "idx", split_axis=0, concat_axis=0, tiled=True
    ).reshape(slots, pick_count)

    images3 = images.reshape(-1, PATCHES, width)
    qkv = qkv_call(images3, norm_gain[None, :], w_qkv)
    embedding, send_rows = attend_call(qkv, w_proj, images3, slot_index[None, :], slots)
    arrived = lax.all_to_all(
        send_rows.reshape(peer_count, capacity, width), "idx", split_axis=0, concat_axis=0, tiled=True
    ).reshape(slots, width)
    chosen = score_call(arrived, got_picks, captions)
    returned = lax.all_to_all(
        chosen.reshape(peer_count, capacity, pick_count * CAPT), "idx", split_axis=0, concat_axis=0, tiled=True
    ).reshape(slots, pick_count * CAPT)
    scores = return_call(slot_index[:, None], returned, pick_count)
    return (embedding, scores)


def solution(mesh):
    placed = (
        P(("rep", "idx"), None),
        P(),
        P(None, "idx"),
        P(),
        P(None, "idx"),
        P(),
        P(("rep", "idx"), None),
        P(("rep", "idx"), None),
        P(("rep", "idx"), None),
    )
    return jax.shard_map(
        local,
        mesh=mesh,
        in_specs=placed,
        out_specs=(P(("rep", "idx"), None), P(("rep", "idx"), None, None)),
        check_vma=False,
    )
```

time: 388 us -> 280 us (0.72)
  local copies, waits for them, and re-layouts: 94.7 us -> 11.3 us
  Pallas kernels: 0 us -> 57.5 us
  other arithmetic: 52.8 us -> 7.14 us
  matrix products: 35.4 us -> 0.35 us
  blocking collectives: 0 us -> 28.1 us
  waiting for transfers between devices: 167 us -> 149 us
  starting transfers between devices: 22 us -> 11.4 us
    pallas_call x0 -> x4, Pallas kernels: none -> 57.5 us  [the longest x1 28.4 us: attend_call(): pl.pallas_call(attend_kernel, in_specs=[full] * 4, out_specs=(full, full)...]
    dot_general x5 -> x1, matrix products: 35.4 us -> 0.35 us  [local(): jnp.dot(dispatch, candidates.astype(BF16), preferred_element_type=F32)]
    all_to_all x0 -> x1, blocking collectives: none -> 28.1 us  [local(): lax.all_to_all(chosen.reshape(peer_count, capacity, pick_count * CAPT), '...]
    gather x4 -> x0, local copies, waits for them, and re-layouts: 26.4 us -> none  [the longest x3 23.3 us: score_slots(): chosen = jnp.take_along_axis(all_scores, block_index[:, :, None], axis=1)]
    all_gather x2 -> x0, local copies, waits for them, and re-layouts: 22.2 us -> none  [the longest x1 16 us: local(): lax.all_gather(qkv_values, 'idx', axis=1, tiled=True)]
    sub x1 -> x0, other arithmetic: 16.6 us -> none  [attend(): logits = logits - jnp.max(logits, axis=-1, keepdims=True)]
    reshape x6 -> x9, local copies, waits for them, and re-layouts: 25.2 us -> 9.17 us  [the longest x1 2.58 us: local(): send_rows.reshape(peer_count, capacity, width)]
    convert_element_type x5 -> x2, other arithmetic: 17.1 us -> 2.31 us  [dequant_rows(): return scaled.reshape(col_count, row_count).astype(BF16)]
  transfers between devices with their start and end apart: 5 -> 4, of which waited for: 4 -> 3; matrix products, arithmetic and copies ran while one was open for 38% -> 4% of each run, Pallas kernels for 0% -> 17%
where the time goes in v1:
time: 280 us; the launch traced here: 279 us
  waiting for transfers between devices  149 us (53%)
  Pallas kernels  57.5 us (21%)
  blocking collectives  28.1 us (10%)
  between operations  14.2 us (5%)
  starting transfers between devices  11.4 us (4%)
  local copies, waits for them, and re-layouts  11.3 us (4%)
  other arithmetic  7.14 us (3%)
    all_gather x1, waiting for transfers between devices, local(): w_qkv = lax.all_gather(qkv_own, 'idx', axis=0, tiled=True)  83.4 us
    all_to_all x1, waiting for transfers between devices, local(): lax.all_to_all(send_rows.reshape(peer_count, capacity, width), 'idx', spl...  34.7 us
    all_gather x1, waiting for transfers between devices, local(): w_proj = lax.all_gather(proj_own, 'idx', axis=0, tiled=True)  30.8 us
    pallas_call x1, Pallas kernels, attend_call(): pl.pallas_call(attend_kernel, in_specs=[full] * 4, out_specs=(full, full)...  28.4 us
    all_to_all x1, blocking collectives, local(): lax.all_to_all(chosen.reshape(peer_count, capacity, pick_count * CAPT), '...  28.1 us
    pallas_call x1, Pallas kernels, qkv_call(): pl.pallas_call(qkv_kernel, grid=(units // step,), in_specs=[pl.BlockSpec(...  19.5 us
    all_to_all x1, starting transfers between devices, local(): lax.all_to_all(send_picks.reshape(peer_count, capacity, pick_count), 'idx...  7.41 us
    pallas_call x1, Pallas kernels, score_call(): pl.pallas_call(score_kernel, in_specs=[full] * 3, out_specs=full, out_sha...  5.95 us
  transfers between devices with their start and end apart: 4, of which 3 were waited for; matrix products, arithmetic and copies ran while one was open for 4% of the time, Pallas kernels for 17%

profile of v1, /device:TPU:0, one launch (start us, length us, event | category | flops | bytes accessed | tf_op | source)
XLA Modules:
  0.0 278.9 jit_solution(1779609190935732926)
XLA Ops:
  7.2 0.9 exponential_bitcast_fusion
  8.2 0.6 mul.54
  8.9 1.4 fusion
  10.4 0.9 exponential_bitcast_fusion.1
  11.6 0.9 fusion.4
  12.6 1.4 reduce-window.6
  14.9 0.6 copy.38
  15.5 7.4 %all-to-all-start.1 = ((bf16[16,34,4]{1,2,0:T(4,128)(2,1)}), bf16[16,34,4]{1,2,0:T(4,128)(2,1)S(1)}, u32[]{:S(2)}, u32[]{:S(2)}) async-start(bf16[16,34,4]{1,2,0:T(4,128)(2,1)} %copy.38), calls=%async_computation.1 | async-start | bytes 32768 | tf_op jit(solution)/shard_map/all_to_all | solution.py:197
  23.1 0.9 reshape_add_fusion
  24.5 1.4 reshape.65.images_ref
  26.6 83.4 %all-gather.3.cloned.1.call-done.w_ref = bf16[4224,1408]{1,0:T(8,128)(2,1)} async-done(((bf16[264,1408]{1,0:T(8,128)(2,1)}), bf16[4224,1408]{1,0:T(8,128)(2,1)}) %all-gather.3.cloned.1.call-update) | async-done | bytes 11894800 | tf_op jit(solution)/shard_map/all_gather | solution.py:184
  110.0 19.5 %qkv.1.qkv_ref = bf16[2,48,88,257]{3,2,1,0:T(8,128)(2,1)} custom-call(bf16[2,257,1408]{2,1,0:T(8,128)(2,1)} %reshape.65.images_ref, f32[1,1408]{1,0:T(1,128)} %broadcast_in_dim.2.gain_ref, bf16[4224,1408]{1,0:T(8,128)(2,1)} %all-gather.3.cloned.1.call-done.w_ref), custom_call_target="tpu_custom_call" | custom-call | tf_op jit(solution)/shard_map/qkv/pallas_call | solution.py:56
  129.4 30.8 %all-gather.5.cloned.1.call-done.proj_ref = bf16[1408,1408]{1,0:T(8,128)(2,1)} async-done(((bf16[88,1408]{1,0:T(8,128)(2,1)}), bf16[1408,1408]{1,0:T(8,128)(2,1)}) %all-gather.5.cloned.1.call-update) | async-done | bytes 3964944 | tf_op jit(solution)/shard_map/all_gather | solution.py:185
  160.2 28.4 %attend.1 = (bf16[514,1408]{1,0:T(8,128)(2,1)}, bf16[544,1408]{1,0:T(8,128)(2,1)}) custom-call(bf16[2,48,88,257]{3,2,1,0:T(8,128)(2,1)} %qkv.1.qkv_ref, bf16[1408,1408]{1,0:T(8,128)(2,1)} %all-gather.5.cloned.1.call-done.proj_ref, bf16[2,257,1408]{2,1,0:T(8,128)(2,1)} %reshape.65.images_ref, s32[1,514]{1,0:T(1,128)} %reshape_add_fusion.1.slot_ref), custom_call_target="tpu_custom_call" | custom-call | tf_op jit(solution)/shard_map/attend/pallas_call | solution.py:104
  188.6 2.6 reshape.68
  191.2 3.9 %all-to-all-start = ((bf16[16,34,1408]{2,1,0:T(8,128)(2,1)}), bf16[16,34,1408]{2,1,0:T(8,128)(2,1)S(1)}, u32[]{:S(2)}, u32[]{:S(2)}) async-start(bf16[16,34,1408]{2,1,0:T(8,128)(2,1)} %reshape.68), calls=%async_computation | async-start | bytes 3604480 | tf_op jit(solution)/shard_map/all_to_all | solution.py:204
  195.2 0.8 copy.40.picks_ref
  196.0 34.7 %all-to-all-done = bf16[16,34,1408]{2,1,0:T(8,128)(2,1)S(1)} async-done(((bf16[16,34,1408]{2,1,0:T(8,128)(2,1)}), bf16[16,34,1408]{2,1,0:T(8,128)(2,1)S(1)}, u32[]{:S(2)}, u32[]{:S(2)}) %all-to-all-start) | async-done | bytes 1531936 | tf_op jit(solution)/shard_map/all_to_all | solution.py:204
  230.7 1.4 reshape.69.rows_ref
  232.1 6.0 %score.1 = bf16[544,512]{1,0:T(8,128)(2,1)} custom-call(bf16[544,1408]{1,0:T(8,128)(2,1)} %reshape.69.rows_ref, bf16[544,4]{1,0:T(8,128)(2,1)} %copy.40.picks_ref, bf16[1024,1408]{1,0:T(8,128)(2,1)} %captions_ref.1), custom_call_target="tpu_custom_call" | custom-call | tf_op jit(solution)/shard_map/score/pallas_call | solution.py:131
  238.0 1.2 reshape.72
  239.2 28.1 %all_to_all.15 = bf16[16,34,512]{2,1,0:T(8,128)(2,1)S(1)} all-to-all(bf16[16,34,512]{2,1,0:T(8,128)(2,1)S(1)} %reshape.72), channel_id=1, replica_groups=mesh['rep'=2,'idx'=16] {'idx'}, dimensions={0} | all-to-all | bytes 1114112 | tf_op jit(solution)/shard_map/all_to_all | solution.py:208
  267.3 1.0 reshape.73.rows_ref
  268.3 3.7 %give_back.1 = bf16[514,4,128]{2,1,0:T(4,128)(2,1)} custom-call(s32[514,1]{1,0:T(8,128)} %get-tuple-element.6.slot_ref, bf16[544,512]{1,0:T(8,128)(2,1)} %reshape.73.rows_ref), custom_call_target="tpu_custom_call" | custom-call | tf_op jit(solution)/shard_map/give_back/pallas_call | solution.py:152
  (35 shorter events, 2.9 us)
Async XLA Ops:
  7.2 1.7 copy-start.1
  7.2 102.8 %all-gather.3.cloned.1.call-start = ((), (), s32[]{:S(2)}) async-start(), calls=%async_computation.3 | async-start | bytes 12638208 | tf_op jit(solution)/shard_map/all_gather | solution.py:184
  10.3 1.3 copy-start.2
  10.3 2.2 copy-start.3
  10.3 4.1 %copy-start.5 = (s32[514,4]{0,1:T(4,128)S(1)}, s32[514,4]{0,1:T(4,128)}, u32[]{:S(2)}) copy-start(s32[514,4]{0,1:T(4,128)} %param.17) | copy-start | bytes 24676
  10.4 149.9 %all-gather.5.cloned.1.call-start = ((), (), s32[]{:S(2)}) async-start(), calls=%async_computation.4 | async-start | bytes 4212736 | tf_op jit(solution)/shard_map/all_gather | solution.py:185
  11.6 12.9 %copy-start = (bf16[514,1408]{1,0:T(8,128)(2,1)S(1)}, bf16[514,1408]{1,0:T(8,128)(2,1)}, u32[]{:S(2)}) copy-start(bf16[514,1408]{1,0:T(8,128)(2,1)} %param.9) | copy-start | bytes 4342276
  15.5 175.7 %all-to-all-start.1 = ((bf16[16,34,4]{1,2,0:T(4,128)(2,1)}), bf16[16,34,4]{1,2,0:T(4,128)(2,1)S(1)}, u32[]{:S(2)}, u32[]{:S(2)}) async-start(bf16[16,34,4]{1,2,0:T(4,128)(2,1)} %copy.38), calls=%async_computation.1 | async-start | bytes 32768 | tf_op jit(solution)/shard_map/all_to_all | solution.py:197
  23.9 2.0 copy-start.4
  191.2 39.5 %all-to-all-start = ((bf16[16,34,1408]{2,1,0:T(8,128)(2,1)}), bf16[16,34,1408]{2,1,0:T(8,128)(2,1)S(1)}, u32[]{:S(2)}, u32[]{:S(2)}) async-start(bf16[16,34,1408]{2,1,0:T(8,128)(2,1)} %reshape.68), calls=%async_computation | async-start | bytes 3604480 | tf_op jit(solution)/shard_map/all_to_all | solution.py:204
Sparse Core Ops, SparseCore 0:
  10.7 99.2 all-gather.2
  112.7 47.5 all-gather.4

commit v2 on v1

--- a/solution.py
+++ b/solution.py
@@ -33,6 +33,235 @@
 
 def dot_nt(left, right):
     return lax.dot_general(left, right, (((1,), (1,)), ((), ())), preferred_element_type=F32)
+
+
+MESH = pl.DeviceIdType.MESH
+SHARE = 11
+
+
+def gather_kernel(q_own, p_own, q_out, p_out, q_hold, p_hold, rz, ry, rx, rc, sz, sy, sx, sc, held):
+    peers = q_out.shape[0]
+    nz = peers // 4
+    me = lax.axis_index("idx")
+    x = lax.axis_index("rep")
+    z, y, c = me // 4, (me // 2) % 2, me % 2
+    own, out = (q_own, p_own), (q_out, p_out)
+
+    def at(zz, yy, cc):
+        return (zz * 2 + yy) * 2 + cc
+
+    to_y, to_c, to_x = (x, at(z, 1 - y, c)), (x, at(z, y, 1 - c)), (1 - x, me)
+    to_up, to_down = (x, me + 4), (x, me - 4)
+
+    barrier = pltpu.get_barrier_semaphore()
+
+    def greet(target):
+        pl.semaphore_signal(barrier, inc=1, device_id=target, device_id_type=MESH)
+
+    for target in (to_y, to_c, to_x):
+        greet(target)
+
+    @pl.when(z + 1 < nz)
+    def _():
+        greet(to_up)
+
+    @pl.when(z > 0)
+    def _():
+        greet(to_down)
+
+    greeted = 3 + jnp.where(z + 1 < nz, 1, 0) + jnp.where(z > 0, 1, 0)
+    pl.semaphore_wait(barrier, greeted)
+
+    def rows(a, k):
+        unit = own[a].shape[0] // SHARE
+        if k == 0:
+            return pl.ds(0, 3 * unit)
+        if k == 3:
+            return pl.ds(0, SHARE * unit)
+        side = x if k == 1 else 1 - x
+        return pl.ds(pl.multiple_of((3 + 4 * side) * unit, 8), 4 * unit)
+
+    def copy(a, shard, k, mine, send, recv, target):
+        span = rows(a, k)
+        return pltpu.make_async_remote_copy(
+            src_ref=own[a].at[span] if mine else out[a].at[shard, span],
+            dst_ref=out[a].at[shard, span],
+            send_sem=send,
+            recv_sem=recv,
+            device_id=target,
+            device_id_type=MESH,
+        )
+
+    def pos(zz, yy):
+        return zz * 2 + yy
+
+    def up(a, zz, k, mine=False):
+        return copy(a, at(zz, y, c), k, mine, sz.at[0, a, zz, k], rz.at[a, zz, k], to_up)
+
+    def down(a, zz, k, mine=False):
+        return copy(a, at(zz, y, c), k, mine, sz.at[1, a, zz, k], rz.at[a, zz, k], to_down)
+
+    def across(a, zz, k, yy, mine=False):
+        return copy(a, at(zz, yy, c), k, mine, sy.at[a, zz, k], ry.at[a, zz, k], to_y)
+
+    def plane(a, zz, yy, k):
+        return copy(a, at(zz, yy, c), k, False, sx.at[a, pos(zz, yy)], rx.at[a, pos(zz, yy)], to_x)
+
+    def core(a, zz, yy, cc, k, mine=False):
+        slot = 0 if k == 3 else k
+        return copy(
+            a, at(zz, yy, cc), k, mine, sc.at[a, pos(zz, yy), slot], rc.at[a, pos(zz, yy), slot], to_c
+        )
+
+    def each(distance, body):
+        if distance == 0:
+            body(z, 0)
+            return
+
+        @pl.when(z - distance >= 0)
+        def _():
+            body(z - distance, -1)
+
+        @pl.when(z + distance < nz)
+        def _():
+            body(z + distance, 1)
+
+    holds = []
+    for a in range(2):
+        for k in (1, 0):
+
+            @pl.when(z + 1 < nz)
+            def _():
+                up(a, z, k, True).start()
+
+            @pl.when(z > 0)
+            def _():
+                down(a, z, k, True).start()
+
+            across(a, z, k, y, True).start()
+        core(a, z, y, c, 3, True).start()
+        hold = (q_hold, p_hold)[a]
+        load = pltpu.make_async_copy(own[a], hold, held.at[a, 0])
+        load.start()
+        holds.append((load, pltpu.make_async_copy(hold, out[a].at[me], held.at[a, 1])))
+    for load, store in holds:
+        load.wait()
+        store.start()
+
+    for a in range(2):
+        for step in range(1, nz + 2):
+            if step < nz:
+
+                def from_chain(zz, side):
+                    for k in (1, 0):
+                        up(a, zz, k).wait_recv()
+                        if side < 0:
+
+                            @pl.when(z + 1 < nz)
+                            def _():
+                                up(a, zz, k).start()
+                        else:
+
+                            @pl.when(z > 0)
+                            def _():
+                                down(a, zz, k).start()
+
+                        across(a, zz, k, y).start()
+                        if k == 1:
+                            plane(a, zz, y, 1).start()
+                        core(a, zz, y, c, k).start()
+
+                each(step, from_chain)
+            if step <= nz:
+
+                def from_across(zz, side):
+                    for k in (1, 0):
+                        across(a, zz, k, 1 - y).wait_recv()
+                        if k == 1:
+                            plane(a, zz, 1 - y, 1).start()
+                        core(a, zz, 1 - y, c, k).start()
+
+                each(step - 1, from_across)
+            if step >= 2:
+
+                def from_plane(zz, side):
+                    if side != 0:
+                        plane(a, zz, y, 2).wait_recv()
+                        core(a, zz, y, c, 2).start()
+                    plane(a, zz, 1 - y, 2).wait_recv()
+                    core(a, zz, 1 - y, c, 2).start()
+
+                each(step - 2, from_plane)
+
+    for a in range(2):
+        for distance in range(nz):
+
+            def finish(zz, side):
+                first = side == 0
+                for k in (1, 0):
+                    if side <= 0:
+
+                        @pl.when(z + 1 < nz)
+                        def _():
+                            up(a, zz, k, first).wait_send()
+
+                    if side >= 0:
+
+                        @pl.when(z > 0)
+                        def _():
+                            down(a, zz, k, first).wait_send()
+
+                    across(a, zz, k, y, first).wait_send()
+                for yy, mine in ((y, first), (1 - y, False)):
+                    if mine:
+                        core(a, zz, yy, c, 3, True).wait_send()
+                        core(a, zz, yy, 1 - c, 3).wait_recv()
+                        continue
+                    plane(a, zz, yy, 1).wait_send()
+                    for k in (1, 0, 2):
+                        core(a, zz, yy, c, k).wait_send()
+                        core(a, zz, yy, 1 - c, k).wait_recv()
+
+            each(distance, finish)
+    for load, store in holds:
+        store.wait()
+
+
+def gather_call(q_own, p_own, peers):
+    anywhere = pl.BlockSpec(memory_space=pl.ANY)
+    nz = peers // 4
+    dma = pltpu.SemaphoreType.DMA
+    return pl.pallas_call(
+        gather_kernel,
+        in_specs=[anywhere] * 2,
+        out_specs=(anywhere, anywhere),
+        out_shape=tuple(jax.ShapeDtypeStruct((peers,) + own.shape, own.dtype) for own in (q_own, p_own)),
+        scratch_shapes=[
+            pltpu.VMEM(q_own.shape, q_own.dtype),
+            pltpu.VMEM(p_own.shape, p_own.dtype),
+            dma((2, nz, 2)),
+            dma((2, nz, 2)),
+            dma((2, 2 * nz)),
+            dma((2, 2 * nz, 3)),
+            dma((2, 2, nz, 2)),
+            dma((2, nz, 2)),
+            dma((2, 2 * nz)),
+            dma((2, 2 * nz, 3)),
+            dma((2, 2)),
+        ],
+        compiler_params=pltpu.CompilerParams(
+            collective_id=0, has_side_effects=True, vmem_limit_bytes=4 * 1024 * 1024
+        ),
+        name="gather_weights",
+    )(q_own, p_own)
+
+
+def gather_rows(q_own, p_own, peers, reps):
+    fits = all(own.shape[0] % (8 * SHARE) == 0 for own in (q_own, p_own))
+    if fits and peers % 8 == 0 and reps == 2:
+        w_qkv, w_proj = gather_call(q_own, p_own, peers)
+        return tuple(w.reshape(-1, w.shape[2]) for w in (w_qkv, w_proj))
+    return tuple(lax.all_gather(own, "idx", axis=0, tiled=True) for own in (q_own, p_own))
 
 
 def qkv_kernel(images_ref, gain_ref, w_ref, out_ref, normed):
@@ -181,8 +410,7 @@
     qkv_cols, proj_cols = qkv_values.shape[1], proj_values.shape[1]
     qkv_own = dequant_rows(qkv_values, own_exponents(qkv_exponents, qkv_cols))
     proj_own = dequant_rows(proj_values, own_exponents(proj_exponents, proj_cols))
-    w_qkv = lax.all_gather(qkv_own, "idx", axis=0, tiled=True)
-    w_proj = lax.all_gather(proj_own, "idx", axis=0, tiled=True)
+    w_qkv, w_proj = gather_rows(qkv_own, proj_own, peer_count, lax.axis_size("rep"))
 
     owner_ids = owners[:, 0]
     onehot = (owner_ids[:, None] == jnp.arange(peer_count, dtype=jnp.int32)[None, :]).astype(

time: 280 us -> 231 us (0.82)
  waiting for transfers between devices: 149 us -> 34.9 us
  Pallas kernels: 57.5 us -> 128 us
  between operations: 14.2 us -> 0.82 us
  local copies, waits for them, and re-layouts: 11.3 us -> 18.6 us
    all_gather x2 -> x0, waiting for transfers between devices: 114 us -> none  [the longest x1 83.4 us: local(): w_qkv = lax.all_gather(qkv_own, 'idx', axis=0, tiled=True)]
    pallas_call x0 -> x1, Pallas kernels: none -> 70.7 us  [gather_call(): pl.pallas_call(gather_kernel, in_specs=[anywhere] * 2, out_specs=(anywher...]
    unnamed x13, local copies, waits for them, and re-layouts: 0.17 us -> 7.54 us
  transfers between devices with their start and end apart: 4 -> 2, of which waited for: 3 -> 1; matrix products, arithmetic and copies ran while one was open for 4% -> 5% of each run, Pallas kernels for 17% -> 52%
where the time goes in v2:
time: 231 us; the launch traced here: 230 us
  Pallas kernels  128 us (55%)
  waiting for transfers between devices  34.9 us (15%)
  blocking collectives  28.1 us (12%)
  local copies, waits for them, and re-layouts  18.6 us (8%)
  starting transfers between devices  11.9 us (5%)
  other arithmetic  6.39 us (3%)
    pallas_call x1, Pallas kernels, gather_call(): pl.pallas_call(gather_kernel, in_specs=[anywhere] * 2, out_specs=(anywher...  70.7 us
    all_to_all x1, waiting for transfers between devices, local(): lax.all_to_all(send_rows.reshape(peer_count, capacity, width), 'idx', spl...  34.9 us
    pallas_call x1, Pallas kernels, attend_call(): pl.pallas_call(attend_kernel, in_specs=[full] * 4, out_specs=(full, full)...  28.4 us
    all_to_all x1, blocking collectives, local(): lax.all_to_all(chosen.reshape(peer_count, capacity, pick_count * CAPT), '...  28.1 us
    pallas_call x1, Pallas kernels, qkv_call(): pl.pallas_call(qkv_kernel, grid=(units // step,), in_specs=[pl.BlockSpec(...  19.4 us
    unnamed x13, local copies, waits for them, and re-layouts  7.54 us
    all_to_all x1, starting transfers between devices, local(): lax.all_to_all(send_picks.reshape(peer_count, capacity, pick_count), 'idx...  7.41 us
    pallas_call x1, Pallas kernels, score_call(): pl.pallas_call(score_kernel, in_specs=[full] * 3, out_specs=full, out_sha...  5.95 us
  transfers between devices with their start and end apart: 2, of which 1 were waited for; matrix products, arithmetic and copies ran while one was open for 5% of the time, Pallas kernels for 52%

profile of v2, /device:TPU:0, one launch (start us, length us, event | category | flops | bytes accessed | tf_op | source)
XLA Modules:
  0.0 229.9 jit_solution(6451164823324769487)
XLA Ops:
  1.4 1.4 reduce-window.6
  3.2 1.1 fusion.2
  5.0 7.4 %all-to-all-start.1 = ((bf16[16,34,4]{1,2,0:T(4,128)(2,1)}), bf16[16,34,4]{1,2,0:T(4,128)(2,1)S(1)}, u32[]{:S(2)}, u32[]{:S(2)}) async-start(bf16[16,34,4]{1,2,0:T(4,128)(2,1)} %copy.38), calls=%async_computation.1 | async-start | bytes 32768 | tf_op jit(solution)/shard_map/all_to_all | solution.py:425
  12.4 0.8 copy.33
  13.2 0.8 exponential_bitcast_fusion
  14.2 0.9 exponential_bitcast_fusion.1
  15.2 0.9 reshape_add_fusion
  16.7 0.8 fusion.q_own
  18.9 1.4 reshape.71.images_ref
  20.9 70.7 %gather_weights.1 = (bf16[16,264,1408]{2,1,0:T(8,128)(2,1)S(1)}, bf16[16,88,1408]{2,1,0:T(8,128)(2,1)S(1)}) custom-call(bf16[264,1408]{1,0:T(8,128)(2,1)S(1)} %fusion.q_own, bf16[88,1408]{1,0:T(8,128)(2,1)S(1)} %fusion.4.p_own), custom_call_target="tpu_custom_call" | custom-call | tf_op jit(solution)/shard_map/gather_weights/pallas_call | solution.py:234
  91.6 4.4 %copy-done = bf16[16,264,1408]{2,1,0:T(8,128)(2,1)} copy-done((bf16[16,264,1408]{2,1,0:T(8,128)(2,1)}, bf16[16,264,1408]{2,1,0:T(8,128)(2,1)S(1)}, u32[]{:S(2)}) %copy-start) | copy-done | bytes 11894808
  96.0 1.9 copy-done.1
  97.9 19.4 %qkv.1.qkv_ref = bf16[2,48,88,257]{3,2,1,0:T(8,128)(2,1)} custom-call(bf16[2,257,1408]{2,1,0:T(8,128)(2,1)} %reshape.71.images_ref, f32[1,1408]{1,0:T(1,128)} %broadcast_in_dim.2.gain_ref, bf16[4224,1408]{1,0:T(8,128)(2,1)} %bitcast.37), custom_call_target="tpu_custom_call" | custom-call | tf_op jit(solution)/shard_map/qkv/pallas_call | solution.py:285
  117.4 28.4 %attend.1 = (bf16[514,1408]{1,0:T(8,128)(2,1)}, bf16[544,1408]{1,0:T(8,128)(2,1)}) custom-call(bf16[2,48,88,257]{3,2,1,0:T(8,128)(2,1)} %qkv.1.qkv_ref, bf16[1408,1408]{1,0:T(8,128)(2,1)} %bitcast.38, bf16[2,257,1408]{2,1,0:T(8,128)(2,1)} %reshape.71.images_ref, s32[1,514]{1,0:T(1,128)} %reshape_add_fusion.1.slot_ref), custom_call_target="tpu_custom_call" | custom-call | tf_op jit(solution)/shard_map/attend/pallas_call | solution.py:333
  145.7 2.6 %reshape.76 = bf16[16,34,1408]{2,1,0:T(8,128)(2,1)} reshape(bf16[544,1408]{1,0:T(8,128)(2,1)} %get-tuple-element.9) | data formatting | bytes 3063808 | tf_op jit(solution)/shard_map/reshape | solution.py:433
  148.3 4.5 %all-to-all-start = ((bf16[16,34,1408]{2,1,0:T(8,128)(2,1)}), bf16[16,34,1408]{2,1,0:T(8,128)(2,1)S(1)}, u32[]{:S(2)}, u32[]{:S(2)}) async-start(bf16[16,34,1408]{2,1,0:T(8,128)(2,1)} %reshape.76), calls=%async_computation | async-start | bytes 3604480 | tf_op jit(solution)/shard_map/all_to_all | solution.py:432
  152.9 0.8 copy.40.picks_ref
  153.7 34.9 %all-to-all-done = bf16[16,34,1408]{2,1,0:T(8,128)(2,1)S(1)} async-done(((bf16[16,34,1408]{2,1,0:T(8,128)(2,1)}), bf16[16,34,1408]{2,1,0:T(8,128)(2,1)S(1)}, u32[]{:S(2)}, u32[]{:S(2)}) %all-to-all-start) | async-done | bytes 1531936 | tf_op jit(solution)/shard_map/all_to_all | solution.py:432
  188.6 1.4 reshape.77.rows_ref
  190.0 6.0 %score.1 = bf16[544,512]{1,0:T(8,128)(2,1)} custom-call(bf16[544,1408]{1,0:T(8,128)(2,1)} %reshape.77.rows_ref, bf16[544,4]{1,0:T(8,128)(2,1)} %copy.40.picks_ref, bf16[1024,1408]{1,0:T(8,128)(2,1)} %captions_ref.1), custom_call_target="tpu_custom_call" | custom-call | tf_op jit(solution)/shard_map/score/pallas_call | solution.py:360
  195.9 1.2 reshape.80
  197.1 28.1 %all_to_all.15 = bf16[16,34,512]{2,1,0:T(8,128)(2,1)S(1)} all-to-all(bf16[16,34,512]{2,1,0:T(8,128)(2,1)S(1)} %reshape.80), channel_id=1, replica_groups=mesh['rep'=2,'idx'=16] {'idx'}, dimensions={0} | all-to-all | bytes 1114112 | tf_op jit(solution)/shard_map/all_to_all | solution.py:436
  225.3 0.9 reshape.81.rows_ref
  226.2 3.7 %give_back.1 = bf16[514,4,128]{2,1,0:T(4,128)(2,1)} custom-call(s32[514,1]{1,0:T(8,128)} %get-tuple-element.10.slot_ref, bf16[544,512]{1,0:T(8,128)(2,1)} %reshape.81.rows_ref), custom_call_target="tpu_custom_call" | custom-call | tf_op jit(solution)/shard_map/give_back/pallas_call | solution.py:381
  (30 shorter events, 4.7 us)
Async XLA Ops:
  5.0 143.3 %all-to-all-start.1 = ((bf16[16,34,4]{1,2,0:T(4,128)(2,1)}), bf16[16,34,4]{1,2,0:T(4,128)(2,1)S(1)}, u32[]{:S(2)}, u32[]{:S(2)}) async-start(bf16[16,34,4]{1,2,0:T(4,128)(2,1)} %copy.38), calls=%async_computation.1 | async-start | bytes 32768 | tf_op jit(solution)/shard_map/all_to_all | solution.py:425
  14.1 2.6 %copy-start.3 = (bf16[1408,264]{0,1:T(8,128)(2,1)S(1)}, bf16[1408,264]{0,1:T(8,128)(2,1)}, u32[]{:S(2)}) copy-start(bf16[1408,264]{0,1:T(8,128)(2,1)} %param.11) | copy-start | bytes 2230276
  16.7 1.0 copy-start.4
  17.5 1.4 copy-start.2
  17.9 2.4 %copy-start.5 = (f32[1408]{0:T(1024)S(1)}, f32[1408]{0:T(1024)}, u32[]{:S(2)}) copy-start(f32[1408]{0:T(1024)} %param.10) | copy-start | bytes 16900
  91.6 4.4 %copy-start = (bf16[16,264,1408]{2,1,0:T(8,128)(2,1)}, bf16[16,264,1408]{2,1,0:T(8,128)(2,1)S(1)}, u32[]{:S(2)}) copy-start(bf16[16,264,1408]{2,1,0:T(8,128)(2,1)S(1)} %get-tuple-element.6) | copy-start | bytes 35684356
  96.0 1.9 copy-start.1
  148.3 40.3 %all-to-all-start = ((bf16[16,34,1408]{2,1,0:T(8,128)(2,1)}), bf16[16,34,1408]{2,1,0:T(8,128)(2,1)S(1)}, u32[]{:S(2)}, u32[]{:S(2)}) async-start(bf16[16,34,1408]{2,1,0:T(8,128)(2,1)} %reshape.76), calls=%async_computation | async-start | bytes 3604480 | tf_op jit(solution)/shard_map/all_to_all | solution.py:432

commit v3 on v2

--- a/solution.py
+++ b/solution.py
@@ -1,4 +1,4 @@
-import functools
+import math
 import jax
 import jax.numpy as jnp
 from jax import lax
@@ -320,14 +320,20 @@
         hidden = images_ref[g].astype(F32) + dot_nt(left, proj_ref[...])
         inv_scale = lax.rsqrt(jnp.mean(hidden * hidden, axis=-1, keepdims=True) + 1e-06)
         emb_ref[g * patches:(g + 1) * patches, :] = (hidden * inv_scale).astype(BF16)
-    slots = send_ref.shape[0]
+    slots = math.prod(send_ref.shape[:-1])
     tokens = group * patches
     pick = lax.broadcasted_iota(jnp.int32, (slots, tokens), 0) == slot_ref[...]
     onehot = jnp.where(pick, 1.0, 0.0).astype(BF16)
-    send_ref[...] = jnp.dot(onehot, emb_ref[...], preferred_element_type=F32).astype(BF16)
-
-
-def attend_call(qkv, w_proj, images3, slot_row, slots):
+    sent = jnp.dot(onehot, emb_ref[...], preferred_element_type=F32).astype(BF16)
+    if len(send_ref.shape) == 2:
+        send_ref[...] = sent
+        return
+    peers, capacity = send_ref.shape[0], send_ref.shape[1]
+    for p in range(peers):
+        send_ref[p] = sent[p * capacity:(p + 1) * capacity]
+
+
+def attend_call(qkv, w_proj, images3, slot_row, slot_shape):
     group, patches, width = images3.shape
     full = pl.BlockSpec(memory_space=VMEM)
     return pl.pallas_call(
@@ -336,7 +342,7 @@
         out_specs=(full, full),
         out_shape=(
             jax.ShapeDtypeStruct((group * patches, width), BF16),
-            jax.ShapeDtypeStruct((slots, width), BF16),
+            jax.ShapeDtypeStruct(slot_shape + (width,), BF16),
         ),
         scratch_shapes=[pltpu.VMEM((width, patches), F32)],
         compiler_params=pltpu.CompilerParams(vmem_limit_bytes=VLIMIT),
@@ -367,11 +373,113 @@
     )(rows, picks, captions)
 
 
-def return_kernel(slot_ref, rows_ref, out_ref):
-    tokens, slots = out_ref.shape[0], rows_ref.shape[0]
+def stride_of(capacity):
+    return -(-capacity // 8) * 8
+
+
+def exchange_kernel(
+    rows_ref, picks_ref, captions_ref, got_ref,
+    rows_in, picks_in, flat, every, chosen, rs, rr, ps, pr, bs, br, own_sem,
+):
+    peers, capacity = rows_ref.shape[0], rows_ref.shape[1]
+    stride = flat.shape[0] // peers
+    pick_count = chosen.shape[2] // CAPT
+    me = lax.axis_index("idx")
+    rep = lax.axis_index("rep")
+
+    def other(step):
+        return (me + step) % peers
+
+    barrier = pltpu.get_barrier_semaphore()
+    for step in range(1, peers):
+        pl.semaphore_signal(barrier, inc=1, device_id=(rep, other(step)), device_id_type=MESH)
+    pl.semaphore_wait(barrier, peers - 1)
+
+    def send(src, dst, send_sems, recv_sems, step):
+        return pltpu.make_async_remote_copy(
+            src_ref=src.at[other(step)],
+            dst_ref=dst.at[me],
+            send_sem=send_sems.at[step],
+            recv_sem=recv_sems.at[step],
+            device_id=(rep, other(step)),
+            device_id_type=MESH,
+        )
+
+    order = sorted(range(1, peers), key=lambda step: -min(step, peers - step))
+    for step in order:
+        send(rows_ref, rows_in, rs, rr, step).start()
+    for step in order:
+        send(picks_ref, picks_in, ps, pr, step).start()
+    own_rows = pltpu.make_async_copy(rows_ref.at[me], rows_in.at[me], own_sem.at[0])
+    own_picks = pltpu.make_async_copy(picks_ref.at[me], picks_in.at[me], own_sem.at[1])
+    own_rows.start()
+    own_picks.start()
+    own_rows.wait()
+    own_picks.wait()
+    for step in order:
+        send(rows_ref, rows_in, rs, rr, step).wait()
+        send(picks_ref, picks_in, ps, pr, step).wait()
+    for p in range(peers):
+        flat[p * stride:p * stride + capacity, :] = rows_in[p]
+    every[...] = dot_nt(flat[...], captions_ref[...])
+    for p in range(peers):
+        columns = picks_in[p].astype(F32).T
+        span = slice(p * stride, p * stride + capacity)
+        for k in range(pick_count):
+            pick = columns[:capacity, k:k + 1]
+            best = jnp.zeros((capacity, CAPT), F32)
+            for b in range(CBLK):
+                best = jnp.where(pick == float(b), every[span, b * CAPT:(b + 1) * CAPT], best)
+            chosen[p, :, k * CAPT:(k + 1) * CAPT] = best.astype(BF16)
+    for step in order:
+        send(chosen, got_ref, bs, br, step).start()
+    own_back = pltpu.make_async_copy(chosen.at[me], got_ref.at[me], own_sem.at[2])
+    own_back.start()
+    own_back.wait()
+    for step in order:
+        send(chosen, got_ref, bs, br, step).wait()
+
+
+def exchange_call(rows, picks, captions, pick_count):
+    peers, capacity, width = rows.shape
+    full = pl.BlockSpec(memory_space=VMEM)
+    flat = peers * stride_of(capacity)
+    dma = pltpu.SemaphoreType.DMA
+    return pl.pallas_call(
+        exchange_kernel,
+        in_specs=[full] * 3,
+        out_specs=pl.BlockSpec(memory_space=pl.ANY),
+        out_shape=jax.ShapeDtypeStruct((peers, capacity, pick_count * CAPT), BF16),
+        scratch_shapes=[
+            pltpu.VMEM(rows.shape, BF16),
+            pltpu.VMEM(picks.shape, BF16),
+            pltpu.VMEM((flat, width), BF16),
+            pltpu.VMEM((flat, captions.shape[0]), F32),
+            pltpu.VMEM((peers, capacity, pick_count * CAPT), BF16),
+        ]
+        + [dma((peers,))] * 6
+        + [dma((3,))],
+        compiler_params=pltpu.CompilerParams(
+            collective_id=1, has_side_effects=True, vmem_limit_bytes=VLIMIT
+        ),
+        name="exchange",
+    )(rows, picks, captions)
+
+
+def return_kernel(slot_ref, rows_ref, out_ref, *packed):
+    if packed:
+        (flat,) = packed
+        flat[...] = jnp.zeros_like(flat)
+        stride = flat.shape[0] // rows_ref.shape[0]
+        for p in range(rows_ref.shape[0]):
+            flat[p * stride:p * stride + rows_ref.shape[1], :] = rows_ref[p]
+        rows = flat[...]
+    else:
+        rows = rows_ref[...]
+    tokens, slots = out_ref.shape[0], rows.shape[0]
     pick = lax.broadcasted_iota(jnp.int32, (tokens, slots), 1) == slot_ref[...]
     onehot = jnp.where(pick, 1.0, 0.0).astype(BF16)
-    got = jnp.dot(onehot, rows_ref[...], preferred_element_type=F32).astype(BF16)
+    got = jnp.dot(onehot, rows, preferred_element_type=F32).astype(BF16)
     for k in range(out_ref.shape[1]):
         out_ref[:, k, :] = got[:, k * CAPT:(k + 1) * CAPT]
 
@@ -383,6 +491,9 @@
         in_specs=[full] * 2,
         out_specs=full,
         out_shape=jax.ShapeDtypeStruct((slot_col.shape[0], pick_count, CAPT), BF16),
+        scratch_shapes=[pltpu.VMEM((rows.shape[0] * stride_of(rows.shape[1]), rows.shape[2]), BF16)]
+        if rows.ndim == 3
+        else [],
         compiler_params=pltpu.CompilerParams(vmem_limit_bytes=VLIMIT),
         name="give_back",
     )(slot_col, rows)
@@ -422,21 +533,27 @@
     pick_count = candidates.shape[1]
     dispatch = (jnp.arange(slots, dtype=jnp.int32)[:, None] == slot_index[None, :]).astype(BF16)
     send_picks = jnp.dot(dispatch, candidates.astype(BF16), preferred_element_type=F32).astype(BF16)
-    got_picks = lax.all_to_all(
-        send_picks.reshape(peer_count, capacity, pick_count), "idx", split_axis=0, concat_axis=0, tiled=True
-    ).reshape(slots, pick_count)
-
     images3 = images.reshape(-1, PATCHES, width)
     qkv = qkv_call(images3, norm_gain[None, :], w_qkv)
-    embedding, send_rows = attend_call(qkv, w_proj, images3, slot_index[None, :], slots)
-    arrived = lax.all_to_all(
-        send_rows.reshape(peer_count, capacity, width), "idx", split_axis=0, concat_axis=0, tiled=True
-    ).reshape(slots, width)
-    chosen = score_call(arrived, got_picks, captions)
-    returned = lax.all_to_all(
-        chosen.reshape(peer_count, capacity, pick_count * CAPT), "idx", split_axis=0, concat_axis=0, tiled=True
-    ).reshape(slots, pick_count * CAPT)
-    scores = return_call(slot_index[:, None], returned, pick_count)
+    if capacity >= 16:
+        turned = send_picks.reshape(peer_count, capacity, pick_count).transpose(0, 2, 1)
+        turned = jnp.pad(turned, ((0, 0), (0, 16 - pick_count), (0, 128 - capacity)))
+        embedding, send_rows = attend_call(
+            qkv, w_proj, images3, slot_index[None, :], (peer_count, capacity)
+        )
+        returned = exchange_call(send_rows, turned, captions, pick_count)
+        place = owner_ids * stride_of(capacity) + slot_rank
+    else:
+        embedding, send_rows = attend_call(qkv, w_proj, images3, slot_index[None, :], (slots,))
+
+        def swap(blocks):
+            shaped = blocks.reshape(peer_count, capacity, blocks.shape[1])
+            moved = lax.all_to_all(shaped, "idx", split_axis=0, concat_axis=0, tiled=True)
+            return moved.reshape(blocks.shape)
+
+        returned = swap(score_call(swap(send_rows), swap(send_picks), captions))
+        place = slot_index
+    scores = return_call(place[:, None], returned, pick_count)
     return (embedding, scores)
 
 

time: 231 us -> 207 us (0.90)
  Pallas kernels: 128 us -> 189 us
  waiting for transfers between devices: 34.9 us -> 0 us
  blocking collectives: 28.1 us -> 0 us
  starting transfers between devices: 11.9 us -> 0 us
  local copies, waits for them, and re-layouts: 18.6 us -> 11.3 us
    pallas_call x1, Pallas kernels: 5.95 us -> 66.2 us  [exchange_call(): pl.pallas_call(exchange_kernel, in_specs=[full] * 3, out_specs=pl.BlockSp...]
    all_to_all x2 -> x0, waiting for transfers between devices: 34.9 us -> none  [the longest x1 34.9 us: local(): lax.all_to_all(send_rows.reshape(peer_count, capacity, width), 'idx', spl...]
    all_to_all x1 -> x0, blocking collectives: 28.1 us -> none  [local(): lax.all_to_all(chosen.reshape(peer_count, capacity, pick_count * CAPT), '...]
    all_to_all x2 -> x0, starting transfers between devices: 11.9 us -> none  [the longest x1 7.41 us: local(): lax.all_to_all(send_picks.reshape(peer_count, capacity, pick_count), 'idx...]
    reshape x8 -> x2, local copies, waits for them, and re-layouts: 7.73 us -> 0.11 us  [local(): send_picks.reshape(peer_count, capacity, pick_count).transpose(0, 2, 1)]
    unnamed x13 -> x16, local copies, waits for them, and re-layouts: 7.54 us -> 6.37 us
  transfers between devices with their start and end apart: 2 -> 0, of which waited for: 1 -> 0; matrix products, arithmetic and copies ran while one was open for 5% -> 0% of each run, Pallas kernels for 52% -> 0%
where the time goes in v3:
time: 207 us
  Pallas kernels  189 us (91%)
  local copies, waits for them, and re-layouts  11.3 us (5%)
  other arithmetic  4.86 us (2%)
    pallas_call x1, Pallas kernels, gather_call(): pl.pallas_call(gather_kernel, in_specs=[anywhere] * 2, out_specs=(anywher...  71.5 us
    pallas_call x1, Pallas kernels, exchange_call(): pl.pallas_call(exchange_kernel, in_specs=[full] * 3, out_specs=pl.BlockSp...  66.2 us
    pallas_call x1, Pallas kernels, attend_call(): pl.pallas_call(attend_kernel, in_specs=[full] * 4, out_specs=(full, full)...  28.5 us
    pallas_call x1, Pallas kernels, qkv_call(): pl.pallas_call(qkv_kernel, grid=(units // step,), in_specs=[pl.BlockSpec(...  19.4 us
    unnamed x16, local copies, waits for them, and re-layouts  6.37 us

profile of v3, /device:TPU:0, one launch (start us, length us, event | category | flops | bytes accessed | tf_op | source)
XLA Modules:
  0.0 206.7 jit_solution(4671851463683808132)
XLA Ops:
  0.6 0.9 exponential_bitcast_fusion
  1.6 0.1 copy.23
  1.7 0.6 mul.60
  2.3 0.8 fusion.q_own
  3.1 0.8 exponential_bitcast_fusion.1
  3.9 0.1 copy.24
  4.0 0.2 mul.64
  4.3 0.2 fusion.4.p_own
  4.5 71.5 %gather_weights.1 = (bf16[16,264,1408]{2,1,0:T(8,128)(2,1)S(1)}, bf16[16,88,1408]{2,1,0:T(8,128)(2,1)S(1)}) custom-call(bf16[264,1408]{1,0:T(8,128)(2,1)S(1)} %fusion.q_own, bf16[88,1408]{1,0:T(8,128)(2,1)S(1)} %fusion.4.p_own), custom_call_target="tpu_custom_call" | custom-call | tf_op jit(solution)/shard_map/gather_weights/pallas_call | solution.py:234
  76.0 4.4 %copy-done = bf16[16,264,1408]{2,1,0:T(8,128)(2,1)} copy-done((bf16[16,264,1408]{2,1,0:T(8,128)(2,1)}, bf16[16,264,1408]{2,1,0:T(8,128)(2,1)S(1)}, u32[]{:S(2)}) %copy-start) | copy-done | bytes 11894808
  80.4 1.9 copy-done.1
  82.3 1.4 reshape.56.images_ref
  83.8 0.6 broadcast_in_dim.2.gain_ref
  84.4 19.4 %qkv.1.qkv_ref = bf16[2,48,88,257]{3,2,1,0:T(8,128)(2,1)} custom-call(bf16[2,257,1408]{2,1,0:T(8,128)(2,1)} %reshape.56.images_ref, f32[1,1408]{1,0:T(1,128)} %broadcast_in_dim.2.gain_ref, bf16[4224,1408]{1,0:T(8,128)(2,1)} %bitcast.40), custom_call_target="tpu_custom_call" | custom-call | tf_op jit(solution)/shard_map/qkv/pallas_call | solution.py:285
  103.8 1.4 reduce-window.6
  105.3 0.2 slice_reduce_fusion
  105.7 0.6 bitcast_add_fusion.slot_ref
  106.3 28.5 %attend.1 = (bf16[514,1408]{1,0:T(8,128)(2,1)}, bf16[16,34,1408]{2,1,0:T(8,128)(2,1)}) custom-call(bf16[2,48,88,257]{3,2,1,0:T(8,128)(2,1)} %qkv.1.qkv_ref, bf16[1408,1408]{1,0:T(8,128)(2,1)} %bitcast.41, bf16[2,257,1408]{2,1,0:T(8,128)(2,1)} %reshape.56.images_ref, s32[1,514]{1,0:T(1,128)} %bitcast_add_fusion.slot_ref), custom_call_target="tpu_custom_call" | custom-call | tf_op jit(solution)/shard_map/attend/pallas_call | solution.py:339
  134.7 0.3 fusion.2
  135.1 0.1 reshape.61
  135.2 0.6 pad.9.picks_ref
  135.9 66.2 %exchange.1.rows_ref = bf16[16,34,512]{2,1,0:T(8,128)(2,1)} custom-call(bf16[16,34,1408]{2,1,0:T(8,128)(2,1)} %get-tuple-element.9.rows_ref, bf16[16,16,128]{2,1,0:T(8,128)(2,1)} %pad.9.picks_ref, bf16[1024,1408]{1,0:T(8,128)(2,1)} %captions_ref.1), custom_call_target="tpu_custom_call" | custom-call | tf_op jit(solution)/shard_map/exchange/pallas_call | solution.py:448
  202.0 0.9 copy.28.slot_ref
  202.9 3.8 %give_back.1 = bf16[514,4,128]{2,1,0:T(4,128)(2,1)} custom-call(s32[514,1]{1,0:T(8,128)} %copy.28.slot_ref, bf16[16,34,512]{2,1,0:T(8,128)(2,1)} %exchange.1.rows_ref), custom_call_target="tpu_custom_call" | custom-call | tf_op jit(solution)/shard_map/give_back/pallas_call | solution.py:489
  (23 shorter events, 0.2 us)
Async XLA Ops:
  0.6 1.7 copy-start.3
  2.3 1.9 copy-start.4
  4.0 78.3 %copy-start.2 = (bf16[514,1408]{1,0:T(8,128)(2,1)S(1)}, bf16[514,1408]{1,0:T(8,128)(2,1)}, u32[]{:S(2)}) copy-start(bf16[514,1408]{1,0:T(8,128)(2,1)} %param.9) | copy-start | bytes 4342276
  76.0 4.4 %copy-start = (bf16[16,264,1408]{2,1,0:T(8,128)(2,1)}, bf16[16,264,1408]{2,1,0:T(8,128)(2,1)S(1)}, u32[]{:S(2)}) copy-start(bf16[16,264,1408]{2,1,0:T(8,128)(2,1)S(1)} %get-tuple-element.6) | copy-start | bytes 35684356
  80.4 1.9 copy-start.1
  82.3 1.4 copy-start.6
  84.4 19.4 %copy-start.5 = (s32[514,1]{0,1:T(1,128)S(1)}, s32[514,1]{0,1:T(1,128)}, u32[]{:S(2)}) copy-start(s32[514,1]{0,1:T(1,128)} %param.16) | copy-start | bytes 6172
  106.3 28.5 %copy-start.7 = (s32[514,4]{0,1:T(4,128)S(1)}, s32[514,4]{0,1:T(4,128)}, u32[]{:S(2)}) copy-start(s32[514,4]{0,1:T(4,128)} %param.17) | copy-start | bytes 24676

commit v4 on v3

--- a/solution.py
+++ b/solution.py
@@ -269,16 +269,19 @@
 
     @pl.when(pl.program_id(0) == 0)
     def _():
-        for g in range(group):
-            normed[g] = layer_norm(images_ref[g], gain_ref[...])
-
+        normed[...] = layer_norm(images_ref[...], gain_ref[...])
+
+    patches = out_ref.shape[3]
+    every = dot_nt(w_ref[...], normed[...])
     for g in range(group):
-        rows = dot_nt(w_ref[...], normed[g])
-        out_ref[g] = rows.reshape(unit, head_dim, rows.shape[1]).astype(BF16)
-
-
-def qkv_call(images3, gain, w_rows):
-    group, patches, width = images3.shape
+        rows = every[:, g * patches:(g + 1) * patches]
+        out_ref[g] = rows.reshape(unit, head_dim, patches).astype(BF16)
+
+
+def qkv_call(images, gain, w_rows):
+    tokens, width = images.shape
+    patches = PATCHES
+    group = tokens // patches
     head_dim = width // HEADS
     units = w_rows.shape[0] // head_dim
     step = 4
@@ -286,16 +289,16 @@
         qkv_kernel,
         grid=(units // step,),
         in_specs=[
-            pl.BlockSpec((group, patches, width), lambda i: (0, 0, 0)),
+            pl.BlockSpec((tokens, width), lambda i: (0, 0)),
             pl.BlockSpec((1, width), lambda i: (0, 0)),
             pl.BlockSpec((step * head_dim, width), lambda i: (i, 0)),
         ],
         out_specs=pl.BlockSpec((group, step, head_dim, patches), lambda i: (0, i, 0, 0)),
         out_shape=jax.ShapeDtypeStruct((group, units, head_dim, patches), BF16),
-        scratch_shapes=[pltpu.VMEM((group, patches, width), BF16)],
+        scratch_shapes=[pltpu.VMEM((tokens, width), BF16)],
         compiler_params=pltpu.CompilerParams(vmem_limit_bytes=VLIMIT),
         name="qkv",
-    )(images3, gain, w_rows)
+    )(images, gain, w_rows)
 
 
 def attend_kernel(qkv_ref, proj_ref, images_ref, slot_ref, emb_ref, send_ref, mixed):
@@ -304,7 +307,7 @@
     scale = head_dim ** (-0.5)
     for g in range(group):
 
-        @pl.loop(0, HEADS)
+        @pl.loop(0, HEADS, unroll=4)
         def _(h):
             queries, keys, vals = qkv_ref[g, h], qkv_ref[g, HEADS + h], qkv_ref[g, 2 * HEADS + h]
             logits = lax.dot_general(
@@ -317,7 +320,7 @@
             mixed[pl.ds(pl.multiple_of(h * head_dim, 8), head_dim), :] = out
 
         left = mixed[...].T.astype(BF16)
-        hidden = images_ref[g].astype(F32) + dot_nt(left, proj_ref[...])
+        hidden = images_ref[g * patches:(g + 1) * patches, :].astype(F32) + dot_nt(left, proj_ref[...])
         inv_scale = lax.rsqrt(jnp.mean(hidden * hidden, axis=-1, keepdims=True) + 1e-06)
         emb_ref[g * patches:(g + 1) * patches, :] = (hidden * inv_scale).astype(BF16)
     slots = math.prod(send_ref.shape[:-1])
@@ -333,8 +336,10 @@
         send_ref[p] = sent[p * capacity:(p + 1) * capacity]
 
 
-def attend_call(qkv, w_proj, images3, slot_row, slot_shape):
-    group, patches, width = images3.shape
+def attend_call(qkv, w_proj, images, slot_row, slot_shape):
+    tokens, width = images.shape
+    patches = qkv.shape[3]
+    group = tokens // patches
     full = pl.BlockSpec(memory_space=VMEM)
     return pl.pallas_call(
         attend_kernel,
@@ -347,7 +352,7 @@
         scratch_shapes=[pltpu.VMEM((width, patches), F32)],
         compiler_params=pltpu.CompilerParams(vmem_limit_bytes=VLIMIT),
         name="attend",
-    )(qkv, w_proj, images3, slot_row)
+    )(qkv, w_proj, images, slot_row)
 
 
 def score_kernel(rows_ref, picks_ref, captions_ref, out_ref):
@@ -533,18 +538,17 @@
     pick_count = candidates.shape[1]
     dispatch = (jnp.arange(slots, dtype=jnp.int32)[:, None] == slot_index[None, :]).astype(BF16)
     send_picks = jnp.dot(dispatch, candidates.astype(BF16), preferred_element_type=F32).astype(BF16)
-    images3 = images.reshape(-1, PATCHES, width)
-    qkv = qkv_call(images3, norm_gain[None, :], w_qkv)
+    qkv = qkv_call(images, norm_gain[None, :], w_qkv)
     if capacity >= 16:
         turned = send_picks.reshape(peer_count, capacity, pick_count).transpose(0, 2, 1)
         turned = jnp.pad(turned, ((0, 0), (0, 16 - pick_count), (0, 128 - capacity)))
         embedding, send_rows = attend_call(
-            qkv, w_proj, images3, slot_index[None, :], (peer_count, capacity)
+            qkv, w_proj, images, slot_index[None, :], (peer_count, capacity)
         )
         returned = exchange_call(send_rows, turned, captions, pick_count)
         place = owner_ids * stride_of(capacity) + slot_rank
     else:
-        embedding, send_rows = attend_call(qkv, w_proj, images3, slot_index[None, :], (slots,))
+        embedding, send_rows = attend_call(qkv, w_proj, images, slot_index[None, :], (slots,))
 
         def swap(blocks):
             shaped = blocks.reshape(peer_count, capacity, blocks.shape[1])

time: 207 us -> 200 us (0.966)
  Pallas kernels: 189 us -> 183 us
    pallas_call x1, Pallas kernels: 28.5 us -> 23.3 us  [attend_call(): pl.pallas_call(attend_kernel, in_specs=[full] * 4, out_specs=(full, full)...]
    unnamed x16 -> x14, local copies, waits for them, and re-layouts: 6.37 us -> 6.37 us
where the time goes in v4:
time: 200 us; the launch traced here: 199 us
  Pallas kernels  183 us (92%)
  local copies, waits for them, and re-layouts  9.91 us (5%)
  other arithmetic  4.86 us (2%)
    pallas_call x1, Pallas kernels, gather_call(): pl.pallas_call(gather_kernel, in_specs=[anywhere] * 2, out_specs=(anywher...  71.5 us
    pallas_call x1, Pallas kernels, exchange_call(): pl.pallas_call(exchange_kernel, in_specs=[full] * 3, out_specs=pl.BlockSp...  66.1 us
    pallas_call x1, Pallas kernels, attend_call(): pl.pallas_call(attend_kernel, in_specs=[full] * 4, out_specs=(full, full)...  23.3 us
    pallas_call x1, Pallas kernels, qkv_call(): pl.pallas_call(qkv_kernel, grid=(units // step,), in_specs=[pl.BlockSpec(...  18.8 us
    unnamed x14, local copies, waits for them, and re-layouts  6.37 us

profile of v4, /device:TPU:0, one launch (start us, length us, event | category | flops | bytes accessed | tf_op | source)
XLA Modules:
  0.0 199.3 jit_solution(1589210549780584424)
XLA Ops:
  0.6 0.9 exponential_bitcast_fusion
  1.6 0.1 copy.23
  1.7 0.6 mul.60
  2.3 0.8 fusion.q_own
  3.1 0.8 exponential_bitcast_fusion.1
  3.9 0.1 copy.24
  4.0 0.3 mul.64
  4.3 0.2 fusion.4.p_own
  4.5 71.5 %gather_weights.1 = (bf16[16,264,1408]{2,1,0:T(8,128)(2,1)S(1)}, bf16[16,88,1408]{2,1,0:T(8,128)(2,1)S(1)}) custom-call(bf16[264,1408]{1,0:T(8,128)(2,1)S(1)} %fusion.q_own, bf16[88,1408]{1,0:T(8,128)(2,1)S(1)} %fusion.4.p_own), custom_call_target="tpu_custom_call" | custom-call | tf_op jit(solution)/shard_map/gather_weights/pallas_call | solution.py:234
  76.0 4.4 %copy-done = bf16[16,264,1408]{2,1,0:T(8,128)(2,1)} copy-done((bf16[16,264,1408]{2,1,0:T(8,128)(2,1)}, bf16[16,264,1408]{2,1,0:T(8,128)(2,1)S(1)}, u32[]{:S(2)}) %copy-start) | copy-done | bytes 11894808
  80.4 1.9 copy-done.1
  82.3 0.6 broadcast_in_dim.2.gain_ref
  82.9 18.8 %qkv.1.qkv_ref = bf16[2,48,88,257]{3,2,1,0:T(8,128)(2,1)} custom-call(bf16[514,1408]{1,0:T(8,128)(2,1)} %images_ref.3, f32[1,1408]{1,0:T(1,128)} %broadcast_in_dim.2.gain_ref, bf16[4224,1408]{1,0:T(8,128)(2,1)} %bitcast.40), custom_call_target="tpu_custom_call" | custom-call | tf_op jit(solution)/shard_map/qkv/pallas_call | solution.py:288
  101.7 1.4 reduce-window.6
  103.2 0.2 slice_reduce_fusion
  103.4 0.1 bitcast_bitcast_fusion
  103.6 0.6 bitcast_add_fusion.slot_ref
  104.1 23.3 %attend.1 = (bf16[514,1408]{1,0:T(8,128)(2,1)}, bf16[16,34,1408]{2,1,0:T(8,128)(2,1)}) custom-call(bf16[2,48,88,257]{3,2,1,0:T(8,128)(2,1)} %qkv.1.qkv_ref, bf16[1408,1408]{1,0:T(8,128)(2,1)} %bitcast.41, bf16[514,1408]{1,0:T(8,128)(2,1)} %images_ref.3, s32[1,514]{1,0:T(1,128)} %bitcast_add_fusion.slot_ref), custom_call_target="tpu_custom_call" | custom-call | tf_op jit(solution)/shard_map/attend/pallas_call | solution.py:344
  127.4 0.3 fusion.2
  127.8 0.1 reshape.57
  127.9 0.6 pad.9.picks_ref
  128.5 66.1 %exchange.1.rows_ref = bf16[16,34,512]{2,1,0:T(8,128)(2,1)} custom-call(bf16[16,34,1408]{2,1,0:T(8,128)(2,1)} %get-tuple-element.9.rows_ref, bf16[16,16,128]{2,1,0:T(8,128)(2,1)} %pad.9.picks_ref, bf16[1024,1408]{1,0:T(8,128)(2,1)} %captions_ref.1), custom_call_target="tpu_custom_call" | custom-call | tf_op jit(solution)/shard_map/exchange/pallas_call | solution.py:453
  194.7 0.9 copy.28.slot_ref
  195.6 3.8 %give_back.1 = bf16[514,4,128]{2,1,0:T(4,128)(2,1)} custom-call(s32[514,1]{1,0:T(8,128)} %copy.28.slot_ref, bf16[16,34,512]{2,1,0:T(8,128)(2,1)} %exchange.1.rows_ref), custom_call_target="tpu_custom_call" | custom-call | tf_op jit(solution)/shard_map/give_back/pallas_call | solution.py:494
  (20 shorter events, 0.1 us)
Async XLA Ops:
  0.6 1.7 copy-start.2
  2.3 2.0 copy-start.3
  3.1 79.2 %copy-start.5 = (f32[1408]{0:T(1024)S(1)}, f32[1408]{0:T(1024)}, u32[]{:S(2)}) copy-start(f32[1408]{0:T(1024)} %param.10) | copy-start | bytes 16900
  76.0 4.4 %copy-start = (bf16[16,264,1408]{2,1,0:T(8,128)(2,1)}, bf16[16,264,1408]{2,1,0:T(8,128)(2,1)S(1)}, u32[]{:S(2)}) copy-start(bf16[16,264,1408]{2,1,0:T(8,128)(2,1)S(1)} %get-tuple-element.6) | copy-start | bytes 35684356
  80.4 1.9 copy-start.1
  82.9 18.8 %copy-start.4 = (s32[514,1]{0,1:T(1,128)S(1)}, s32[514,1]{0,1:T(1,128)}, u32[]{:S(2)}) copy-start(s32[514,1]{0,1:T(1,128)} %param.16) | copy-start | bytes 6172
  104.1 23.3 %copy-start.6 = (s32[514,4]{0,1:T(4,128)S(1)}, s32[514,4]{0,1:T(4,128)}, u32[]{:S(2)}) copy-start(s32[514,4]{0,1:T(4,128)} %param.17) | copy-start | bytes 24676
